TPU v7x, 32 devices: a whole 2x2x4 slice. The times are simulated.
32 devices in a mesh: dp: 4 (over y, x), fsdp: 8 (over z, core).
Axes of the slice: x: 2, y: 2, z: 4, core: 2. Of those that a mesh axis runs over, the one named last changes fastest.
Arguments:
- tokens_in: bfloat16 [32, 256, 1024], P(('dp', 'fsdp')), may hold values from -6 to 6
- cotangent: bfloat16 [32, 256, 1024], P(('dp', 'fsdp')), may hold values from -6 to 6
- lengths: int32 [32], P(('dp', 'fsdp')), may hold values from 128 to 256
- qkv_master: float32 [1024, 3072], P('fsdp'), may hold values from -0.5625 to 0.5625
- out_master: float32 [1024, 1024], P('fsdp'), may hold values from -2.25 to 2.25
- up_master: float32 [1024, 4096], P('fsdp'), may hold values from -0.5625 to 0.5625
- down_master: float32 [4096, 1024], P('fsdp'), may hold values from -0.28125 to 0.28125
- small_master: float32 [13312], P('fsdp'), may hold values from -0.8 to 1.4
- qkv_first: float32 [1024, 3072], P('fsdp'), may hold values from -814.58701 to 814.58701
- out_first: float32 [1024, 1024], P('fsdp'), may hold values from -407.29351 to 407.29351
- up_first: float32 [1024, 4096], P('fsdp'), may hold values from -814.58701 to 814.58701
- down_first: float32 [4096, 1024], P('fsdp'), may hold values from -814.58701 to 814.58701
- small_first: float32 [13312], P('fsdp'), may hold values from -1629.17402 to 1629.17402
- qkv_second: float32 [1024, 3072], P('fsdp'), may hold values from 2048 to 8192
- out_second: float32 [1024, 1024], P('fsdp'), may hold values from 512 to 2048
- up_second: float32 [1024, 4096], P('fsdp'), may hold values from 2048 to 8192
- down_second: float32 [4096, 1024], P('fsdp'), may hold values from 2048 to 8192
- small_second: float32 [13312], P('fsdp'), may hold values from 8192 to 32768
Outputs:
- output: bfloat16 [32, 256, 1024], P(('dp', 'fsdp'))
- input_grad: bfloat16 [32, 256, 1024], P(('dp', 'fsdp'))
- qkv_new: float32 [1024, 3072], P('fsdp')
- out_new: float32 [1024, 1024], P('fsdp')
- up_new: float32 [1024, 4096], P('fsdp')
- down_new: float32 [4096, 1024], P('fsdp')
- small_new: float32 [13312], P('fsdp')
- qkv_first_new: float32 [1024, 3072], P('fsdp')
- out_first_new: float32 [1024, 1024], P('fsdp')
- up_first_new: float32 [1024, 4096], P('fsdp')
- down_first_new: float32 [4096, 1024], P('fsdp')
- small_first_new: float32 [13312], P('fsdp')
- qkv_second_new: float32 [1024, 3072], P('fsdp')
- out_second_new: float32 [1024, 1024], P('fsdp')
- up_second_new: float32 [1024, 4096], P('fsdp')
- down_second_new: float32 [4096, 1024], P('fsdp')
- small_second_new: float32 [13312], P('fsdp')
- lamb_norms: float32 [2, 5], replicated
All inputs are finite; a program needn't handle non-finite values.
Results may differ from a plain program's by a relative error of at most 0.012.
The roundings to bfloat16 on the way count: a program that leaves them out, or rounds other values in their place, can miss the bound.
Values may be sent and summed in bfloat16 or wider, within the bound.
A program may use at most 256 MiB of HBM per device.

v0:
```python
import math
import jax
import jax.numpy as jnp
from jax import lax
from jax.sharding import PartitionSpec as P

D = 1024
HEADS = 16
HD = 64
FF = 4096
ROT = 16
NORM_EPSILON = 1e-05
ADAM_EPSILON = 1e-06
ROPE_BASE = 10000.0
RATE = 0.5
DECAY = 0.01
BETA_ONE = 0.5
BETA_TWO = 0.5


def split_small(small_vector):
    bounds = [0, D, 2 * D, 3 * D, 4 * D, 7 * D, 8 * D, 8 * D + FF, 9 * D + FF]
    return [small_vector[bounds[number] : bounds[number + 1]] for number in range(8)]


def normalize(values):
    average = jnp.mean(values, axis=-1, keepdims=True)
    centred = values - average
    variance = jnp.mean(centred * centred, axis=-1, keepdims=True)
    inverse = lax.rsqrt(variance + NORM_EPSILON)
    return (centred * inverse, inverse)


def rotary_tables(length):
    half_dims = ROT // 2
    position = jnp.arange(length, dtype=jnp.float32)[:, None]
    number = jnp.arange(half_dims, dtype=jnp.float32)[None, :]
    angle = position * jnp.exp(number * (-2.0 * math.log(ROPE_BASE) / ROT))
    return (jnp.cos(angle)[:, None, :], jnp.sin(angle)[:, None, :])


def rotate(heads_in, cosine_table, sine_table):
    half_dims = ROT // 2
    first_half = heads_in[..., :half_dims]
    second_half = heads_in[..., half_dims:ROT]
    return jnp.concatenate(
        [
            first_half * cosine_table - second_half * sine_table,
            second_half * cosine_table + first_half * sine_table,
            heads_in[..., ROT:],
        ],
        axis=-1,
    )


def rotate_back(grads_in, cosine_table, sine_table):
    half_dims = ROT // 2
    first_half = grads_in[..., :half_dims]
    second_half = grads_in[..., half_dims:ROT]
    return jnp.concatenate(
        [
            first_half * cosine_table + second_half * sine_table,
            second_half * cosine_table - first_half * sine_table,
            grads_in[..., ROT:],
        ],
        axis=-1,
    )


def gelu_slope(values):
    return 0.5 * (1.0 + lax.erf(values * 2.0 ** (-0.5))) + values * jnp.exp(
        -0.5 * values * values
    ) * (2.0 * math.pi) ** (-0.5)


def against(left, right):
    return lax.dot_general(
        left, right, (((1,), (1,)), ((), ())), preferred_element_type=jnp.float32
    )


def outer_sum(columns, right):
    return lax.dot_general(
        columns, right, (((0,), (0,)), ((), ())), preferred_element_type=jnp.float32
    )


def local_squares(arrays):
    return jnp.stack([jnp.sum(array_in * array_in) for array_in in arrays])


def sliced(master, part, parts, pieces):
    rows, columns = master.shape
    width = columns // (pieces * parts)
    return lax.dynamic_index_in_dim(
        master.reshape(rows, pieces, parts, width), part, axis=2, keepdims=False
    ).reshape(rows, pieces * width)


def joined(slices, pieces):
    parts, rows, columns = slices.shape
    width = columns // pieces
    return (
        slices.reshape(parts, rows, pieces, width)
        .transpose(1, 2, 0, 3)
        .reshape(rows, pieces * parts * width)
    )


def layer(x_all, cotangent_all, lengths_all, weights, small_all, part):
    qkv_weight, out_weight, up_weight, down_weight = weights
    group, length, _ = x_all.shape
    tokens = group * length
    head_cols = out_weight.shape[0]
    heads = head_cols // HD
    gain_one, shift_one, gain_two, shift_two, qkv_bias, up_bias = small_all
    inputs = x_all.reshape(tokens, D).astype(jnp.float32)
    position = jnp.arange(length)
    live = (position[None, :] < lengths_all[:, None]).astype(jnp.float32).reshape(tokens, 1)
    allowed = (position[None, None, :] <= position[None, :, None]) & (
        position[None, None, :] < lengths_all[:, None, None]
    )
    unit_rows, _ = normalize(inputs)
    normed_one = (unit_rows * gain_one + shift_one).astype(jnp.bfloat16)
    normed_two = (unit_rows * gain_two + shift_two).astype(jnp.bfloat16)
    projected = jnp.dot(normed_one, qkv_weight, preferred_element_type=jnp.float32) + qkv_bias
    projected = projected.reshape(group, length, 3, heads, HD)
    cosine_table, sine_table = rotary_tables(length)
    query_heads = rotate(projected[:, :, 0], cosine_table, sine_table).astype(jnp.bfloat16)
    key_heads = rotate(projected[:, :, 1], cosine_table, sine_table).astype(jnp.bfloat16)
    value_heads = projected[:, :, 2].astype(jnp.bfloat16)
    scores = jnp.einsum(
        "gqhd,gkhd->ghqk", query_heads, key_heads, preferred_element_type=jnp.float32
    ) * HD ** (-0.5)
    scores = jnp.where(allowed[:, None], scores, -1e30)
    row_top = jnp.max(scores, axis=-1, keepdims=True)
    raised = jnp.exp(scores - row_top)
    attend = raised / jnp.sum(raised, axis=-1, keepdims=True)
    attend_low = attend.astype(jnp.bfloat16)
    mixed = jnp.einsum(
        "ghqk,gkhd->gqhd", attend_low, value_heads, preferred_element_type=jnp.float32
    )
    mixed = mixed.reshape(tokens, head_cols).astype(jnp.bfloat16)
    hidden = jnp.dot(normed_two, up_weight, preferred_element_type=jnp.float32) + up_bias
    activated = jax.nn.gelu(hidden, approximate=False).astype(jnp.bfloat16)
    out_part = jnp.dot(mixed, out_weight, preferred_element_type=jnp.float32) + jnp.dot(
        activated, down_weight, preferred_element_type=jnp.float32
    )
    back = (cotangent_all.reshape(tokens, D).astype(jnp.float32) * live).astype(jnp.bfloat16)
    d_hidden = (against(back, down_weight) * gelu_slope(hidden)).astype(jnp.bfloat16)
    d_mixed = against(back, out_weight).astype(jnp.bfloat16).reshape(group, length, heads, HD)
    d_attend = jnp.einsum(
        "gqhd,gkhd->ghqk", d_mixed, value_heads, preferred_element_type=jnp.float32
    )
    row_inner = jnp.sum(attend * d_attend, axis=-1, keepdims=True)
    d_scores = (attend * (d_attend - row_inner)).astype(jnp.bfloat16)
    d_queries = jnp.einsum(
        "ghqk,gkhd->gqhd", d_scores, key_heads, preferred_element_type=jnp.float32
    ) * HD ** (-0.5)
    d_keys = jnp.einsum(
        "ghqk,gqhd->gkhd", d_scores, query_heads, preferred_element_type=jnp.float32
    ) * HD ** (-0.5)
    d_values = jnp.einsum(
        "ghqk,gqhd->gkhd", attend_low, d_mixed, preferred_element_type=jnp.float32
    )
    d_projected = jnp.stack(
        [
            rotate_back(d_queries, cosine_table, sine_table),
            rotate_back(d_keys, cosine_table, sine_table),
            d_values,
        ],
        axis=2,
    )
    d_projected = d_projected.reshape(tokens, 3 * head_cols).astype(jnp.bfloat16)
    d_normed_one = against(d_projected, qkv_weight)
    d_normed_two = against(d_hidden, up_weight)
    scaled_part = d_normed_one * gain_one + d_normed_two * gain_two
    norm_sums = jnp.stack(
        [
            jnp.sum(d_normed_one * unit_rows, axis=0),
            jnp.sum(d_normed_one, axis=0),
            jnp.sum(d_normed_two * unit_rows, axis=0),
            jnp.sum(d_normed_two, axis=0),
        ]
    )
    d_qkv_bias = jnp.sum(d_projected, axis=0, dtype=jnp.float32)
    d_up_bias = jnp.sum(d_hidden, axis=0, dtype=jnp.float32)
    terms = (
        outer_sum(normed_one, d_projected),
        outer_sum(mixed, back),
        outer_sum(normed_two, d_hidden),
        outer_sum(activated, back),
    )
    return (
        out_part.astype(jnp.bfloat16),
        scaled_part.astype(jnp.bfloat16),
        tuple((term.astype(jnp.bfloat16) for term in terms)),
        (norm_sums, d_qkv_bias, d_up_bias),
    )


def local_split(
    tokens_in,
    cotangent,
    lengths,
    qkv_master,
    out_master,
    up_master,
    down_master,
    small_master,
    qkv_first,
    out_first,
    up_first,
    down_first,
    small_first,
    qkv_second,
    out_second,
    up_second,
    down_second,
    small_second,
):
    masters = (qkv_master, out_master, up_master, down_master, small_master)
    firsts = (qkv_first, out_first, up_first, down_first, small_first)
    seconds = (qkv_second, out_second, up_second, down_second, small_second)
    parts, shards = (lax.axis_size("dp"), lax.axis_size("fsdp"))
    part, shard = (lax.axis_index("dp"), lax.axis_index("fsdp"))
    length = tokens_in.shape[1]
    head_cols = D // parts
    ff_cols = FF // parts
    ff_rows = down_master.shape[0] // parts
    qkv_own = sliced(qkv_master, part, parts, 3).astype(jnp.bfloat16)
    up_own = sliced(up_master, part, parts, shards).astype(jnp.bfloat16)
    down_own = lax.dynamic_slice_in_dim(down_master, part * ff_rows, ff_rows).astype(jnp.bfloat16)
    out_own = out_master.astype(jnp.bfloat16)
    small_own = small_master.astype(jnp.bfloat16)

    def over_shards(own):
        return lax.all_gather(own, "fsdp", axis=0, tiled=True)

    x_all = lax.all_gather(tokens_in, "dp", axis=0, tiled=True)
    cotangent_all = lax.all_gather(cotangent, "dp", axis=0, tiled=True)
    lengths_all = lax.all_gather(lengths, "dp", axis=0, tiled=True)
    qkv_weight, up_weight, down_weight = (over_shards(w) for w in (qkv_own, up_own, down_own))
    out_weight = lax.dynamic_slice_in_dim(over_shards(out_own), part * head_cols, head_cols)
    gain_one, shift_one, gain_two, shift_two, qkv_bias, out_bias, up_bias, down_bias = split_small(
        over_shards(small_own).astype(jnp.float32)
    )
    qkv_bias = sliced(qkv_bias[None], part, parts, 3)[0]
    up_bias = sliced(up_bias[None], part, parts, shards)[0]
    out_part, scaled_part, terms, sums = layer(
        x_all,
        cotangent_all,
        lengths_all,
        (qkv_weight, out_weight, up_weight, down_weight),
        (gain_one, shift_one, gain_two, shift_two, qkv_bias, up_bias),
        part,
    )
    out_sum = lax.psum_scatter(out_part, "dp", scatter_dimension=0, tiled=True)
    scaled = lax.psum_scatter(scaled_part, "dp", scatter_dimension=0, tiled=True)
    out_sum, scaled = (out_sum.astype(jnp.float32), scaled.astype(jnp.float32))
    inputs = tokens_in[0].astype(jnp.float32)
    live = (jnp.arange(length) < lengths[0]).astype(jnp.float32)[:, None]
    back = cotangent[0].astype(jnp.float32) * live
    unit_rows, inverse_rows = normalize(inputs)
    output = ((inputs + out_sum + out_bias + down_bias) * live).astype(jnp.bfloat16)
    input_grad = back + inverse_rows * (
        scaled
        - jnp.mean(scaled, axis=-1, keepdims=True)
        - unit_rows * jnp.mean(scaled * unit_rows, axis=-1, keepdims=True)
    )
    norm_sums, d_qkv_bias, d_up_bias = sums
    back_total = jnp.sum(back, axis=0)

    def spread(values, pieces):
        wide = jnp.zeros((pieces, parts, values.shape[0] // pieces), jnp.float32)
        return lax.dynamic_update_index_in_dim(
            wide, values.reshape(pieces, -1), part, axis=1
        ).reshape(-1)

    small_grad = jnp.concatenate(
        [
            norm_sums.reshape(4 * D),
            spread(d_qkv_bias, 3),
            back_total,
            spread(d_up_bias, shards),
            back_total,
        ]
    )
    small_sum = lax.psum(small_grad, ("dp", "fsdp"))
    small_rows = small_master.shape[0]
    small_sum = lax.dynamic_slice_in_dim(small_sum, shard * small_rows, small_rows)
    qkv_term, out_term, up_term, down_term = terms
    out_wide = lax.dynamic_update_slice_in_dim(
        jnp.zeros((D, D), jnp.bfloat16), out_term, part * head_cols, axis=0
    )

    def to_owner(term):
        own = lax.psum_scatter(term, "fsdp", scatter_dimension=0, tiled=True)
        return lax.all_gather(own, "dp", axis=0, tiled=False).astype(jnp.float32)

    qkv_sum = joined(to_owner(qkv_term), 3)
    up_sum = joined(to_owner(up_term), shards)
    down_sum = to_owner(down_term).reshape(down_master.shape)
    out_sum_grad = lax.psum(
        lax.psum_scatter(out_wide, "fsdp", scatter_dimension=0, tiled=True), "dp"
    ).astype(jnp.float32)
    reduced = (qkv_sum, out_sum_grad, up_sum, down_sum, small_sum)
    return (output[None], input_grad.astype(jnp.bfloat16)[None]) + lamb(
        masters, firsts, seconds, reduced
    )


def lamb(masters, firsts, seconds, reduced):
    updates = []
    first_news = []
    second_news = []
    for first_old, second_old, master, grad_sum in zip(firsts, seconds, masters, reduced):
        first_new = BETA_ONE * first_old + (1.0 - BETA_ONE) * grad_sum
        second_new = BETA_TWO * second_old + (1.0 - BETA_TWO) * grad_sum * grad_sum
        updates.append(first_new / (jnp.sqrt(second_new) + ADAM_EPSILON) + DECAY * master)
        first_news.append(first_new)
        second_news.append(second_new)
    weight_squares, update_squares = lax.psum(
        (local_squares(masters), local_squares(updates)), "fsdp"
    )
    weight_norms = jnp.sqrt(weight_squares)
    update_norms = jnp.sqrt(update_squares)
    new_masters = [
        masters[number] - RATE * (weight_norms[number] / update_norms[number]) * updates[number]
        for number in range(5)
    ]
    lamb_norms = jnp.stack([weight_norms, update_norms])
    return tuple(new_masters) + tuple(first_news) + tuple(second_news) + (lamb_norms,)


def solution(mesh):
    in_specs = (
        P(("dp", "fsdp"), None, None),
        P(("dp", "fsdp"), None, None),
        P(("dp", "fsdp")),
        P("fsdp", None),
        P("fsdp", None),
        P("fsdp", None),
        P("fsdp", None),
        P("fsdp"),
        P("fsdp", None),
        P("fsdp", None),
        P("fsdp", None),
        P("fsdp", None),
        P("fsdp"),
        P("fsdp", None),
        P("fsdp", None),
        P("fsdp", None),
        P("fsdp", None),
        P("fsdp"),
    )
    out_specs = (
        P(("dp", "fsdp"), None, None),
        P(("dp", "fsdp"), None, None),
        P("fsdp", None),
        P("fsdp", None),
        P("fsdp", None),
        P("fsdp", None),
        P("fsdp"),
        P("fsdp", None),
        P("fsdp", None),
        P("fsdp", None),
        P("fsdp", None),
        P("fsdp"),
        P("fsdp", None),
        P("fsdp", None),
        P("fsdp", None),
        P("fsdp", None),
        P("fsdp"),
        P(),
    )
    return jax.shard_map(
        local_split, mesh=mesh, in_specs=in_specs, out_specs=out_specs, check_vma=False
    )
```

profile of v0, /device:TPU:0, one launch (start us, length us, event | category | flops | bytes accessed | tf_op | source)
XLA Modules:
  0.0 634.2 jit_solution(11582230660681982558)
XLA Ops:
  8.0 3.2 copy.87
  17.1 15.7 %all-gather.3 = bf16[8,1,1664]{2,1,0:T(2,128)(2,1)S(1)} all-gather(bf16[1,1,1664]{2,1,0:T(2,128)(2,1)S(1)} %reshape.376), channel_id=1, replica_groups=mesh['dp'=4,'fsdp'=8] {'fsdp'}, dimensions={0}, use_global_device_ids=true | all-gather | bytes 29952 | tf_op jit(solution)/shard_map/all_gather | solution.py:238
  36.3 8.1 %all-reduce = s32[4]{0:T(128)S(1)} all-reduce(s32[4]{0:T(128)S(1)} %dynamic-update-slice), channel_id=1, replica_groups=mesh['dp'=4,'fsdp'=8] {'dp'}, use_global_device_ids=true, to_apply=%add | all-reduce | flops 4 | bytes 32
  51.6 2.8 add_convert_fusion.4
  54.4 23.0 %all-gather.15.cloned.1.call-done = bf16[1024,768]{0,1:T(8,128)(2,1)} async-done(((bf16[128,768]{0,1:T(8,128)(2,1)}), bf16[1024,768]{0,1:T(8,128)(2,1)}) %all-gather.15.cloned.1.call-update) | async-done | bytes 1572880 | tf_op jit(solution)/shard_map/all_gather | solution.py:238
  77.4 5.6 convolution_add_fusion
  82.9 6.4 %reshape.381 = f32[4,256,3,4,64]{4,3,2,1,0:T(4,128)} reshape(f32[1024,768]{1,0:T(8,128)} %convolution_add_fusion) | data formatting | bytes 6291456 | tf_op jit(solution)/shard_map/reshape | solution.py:127
  91.3 4.5 fusion.75
  106.7 5.2 fusion.79
  121.5 3.4 fusion.10
  124.9 21.7 %all-gather.19.cloned.1.call-done = bf16[1024,1024]{0,1:T(8,128)(2,1)} async-done(((bf16[128,1024]{0,1:T(8,128)(2,1)}), bf16[1024,1024]{0,1:T(8,128)(2,1)}) %all-gather.19.cloned.1.call-update) | async-done | bytes 2097168 | tf_op jit(solution)/shard_map/all_gather | solution.py:238
  146.6 14.6 %fusion.3 = (bf16[1024,1024]{1,0:T(8,128)(2,1)}, f32[1024,1024]{1,0:T(8,128)}) fusion(f32[1024]{0:T(1024)S(1)} %bitcast.220, bf16[1024,1024]{1,0:T(8,128)(2,1)} %get-tuple-element.89, bf16[1024,1024]{0,1:T(8,128)(2,1)} %all-gather.19.cloned.1.call-done), kind=kOutput, calls=%fused_computation.5 | convolution fusion | flops 2216689664 | bytes 10489856 | tf_op jit(solution)/shard_map/dot_general | solution.py:144
  161.2 15.7 %all-gather.21.cloned.1.call-done = bf16[1024,1024]{1,0:T(8,128)(2,1)} async-done(((bf16[128,1024]{1,0:T(8,128)(2,1)}), bf16[1024,1024]{1,0:T(8,128)(2,1)}) %all-gather.21.cloned.1.call-update) | async-done | bytes 2097168 | tf_op jit(solution)/shard_map/all_gather | solution.py:238
  176.8 8.0 %convert_reduce_fusion = (f32[1024]{0:T(1024)}, bf16[1024,1024]{1,0:T(8,128)(2,1)}) fusion(f32[1024,1024]{1,0:T(8,128)} %get-tuple-element.138, f32[1024]{0:T(1024)S(1)} %bitcast.221, bf16[1024,1024]{1,0:T(8,128)(2,1)} %fusion.10, bf16[1024,1024]{1,0:T(8,128)(2,1)} %all-gather.21.cloned.1.call-done), kind=kOutput, calls=%fused_computation.16 | convolution fusion | flops 2161114112 | bytes 10493952 | tf_op jit(solution)/shard_map/dot_general | solution.py:77
  184.9 30.0 %reduce-scatter.13.cloned.1.call-done = bf16[128,1024]{1,0:T(8,128)(2,1)} async-done(((bf16[1024,1024]{1,0:T(8,128)(2,1)}), bf16[128,1024]{1,0:T(8,128)(2,1)}) %reduce-scatter.13.cloned.1.call-update) | async-done | bytes 262160 | tf_op jit(solution)/shard_map/reduce_scatter | solution.py:305
  214.9 5.9 convolution_convert_fusion.1
  221.2 6.0 convolution_convert_fusion
  227.2 32.3 %all-reduce.4.cloned.1.call-done = bf16[128,1024]{1,0:T(8,128)(2,1)} async-done(((bf16[128,1024]{1,0:T(8,128)(2,1)}), bf16[128,1024]{1,0:T(8,128)(2,1)}) %all-reduce.4.cloned.1.call-update) | async-done | bytes 262160 | tf_op jit(solution)/shard_map/psum | solution.py:304
  259.5 3.1 multiply_reduce_fusion.10
  262.6 35.6 %reduce-scatter.15.cloned.1.call-done = bf16[128,1024]{1,0:T(8,128)(2,1)} async-done(((bf16[1024,1024]{1,0:T(8,128)(2,1)}), bf16[128,1024]{1,0:T(8,128)(2,1)}) %reduce-scatter.15.cloned.1.call-update) | async-done | bytes 262160 | tf_op jit(solution)/shard_map/reduce_scatter | solution.py:298
  298.3 2.8 add_convert_fusion
  301.2 34.5 %reduce-scatter.17.cloned.1.call-done = bf16[128,1024]{1,0:T(8,128)(2,1)} async-done(((bf16[1024,1024]{1,0:T(8,128)(2,1)}), bf16[128,1024]{1,0:T(8,128)(2,1)}) %reduce-scatter.17.cloned.1.call-update) | async-done | bytes 262160 | tf_op jit(solution)/shard_map/reduce_scatter | solution.py:298
  335.8 29.7 %all-gather.17.cloned.1.call-done = bf16[1024,1024]{1,0:T(8,128)(2,1)} async-done(((bf16[128,1024]{1,0:T(8,128)(2,1)}), bf16[1024,1024]{1,0:T(8,128)(2,1)}) %all-gather.17.cloned.1.call-update) | async-done | bytes 2097168 | tf_op jit(solution)/shard_map/all_gather | solution.py:238
  365.5 3.2 convolution_convert_fusion.4
  372.0 3.6 multiply_reduce_fusion.2
  383.9 3.0 convolution_convert_fusion.2
  387.5 4.7 fusion.81
  392.3 4.3 multiply_reduce_fusion.1
  399.6 3.1 copy.105
  403.1 4.6 fusion.80
  407.7 3.1 add_convert_fusion.2
  419.0 3.3 all-gather.27.cloned.1.call-done
  422.2 7.5 %multiply_reduce_fusion.4 = (f32[]{:T(128)}, f32[]{:T(128)}, f32[512,1024]{1,0:T(8,128)}, f32[512,1024]{1,0:T(8,128)}) fusion(f32[512,1024]{1,0:T(8,128)} %param.24, bf16[512,1024]{1,0:T(8,128)(2,1)} %all-gather.27.cloned.1.call-done, f32[512,1024]{1,0:T(8,128)} %param.34, f32[512,1024]{1,0:T(8,128)} %param.29), kind=kLoop, calls=%fused_computation.61 | loop fusion | flops 7864318 | bytes 11534344 | tf_op jit(solution)/shard_map/reduce_sum | solution.py:89
  429.8 4.1 multiply_reduce_fusion.5
  434.1 25.4 %reduce-scatter.11.cloned.1.call-done = bf16[128,768]{1,0:T(8,128)(2,1)} async-done(((bf16[1024,768]{1,0:T(8,128)(2,1)}), bf16[128,768]{1,0:T(8,128)(2,1)}) %reduce-scatter.11.cloned.1.call-update) | async-done | bytes 196624 | tf_op jit(solution)/shard_map/reduce_scatter | solution.py:298
  459.4 14.9 %all-gather = bf16[512,768]{1,0:T(8,128)(2,1)S(1)} all-gather(bf16[128,768]{1,0:T(8,128)(2,1)} %reduce-scatter.11.cloned.1.call-done), channel_id=2, replica_groups=mesh['dp'=4,'fsdp'=8] {'dp'}, dimensions={0}, use_global_device_ids=true | all-gather | bytes 983040 | tf_op jit(solution)/shard_map/all_gather | solution.py:299
  480.9 4.9 multiply_reduce_fusion.8
  485.8 3.1 copy.110
  488.9 7.5 %reduce-scatter.9.cloned.1.call-done = bf16[256,1024]{1,0:T(8,128)(2,1)} async-done(((bf16[1024,1024]{1,0:T(8,128)(2,1)}), bf16[256,1024]{1,0:T(8,128)(2,1)}) %reduce-scatter.9.cloned.1.call-update) | async-done | bytes 524304 | tf_op jit(solution)/shard_map/reduce_scatter | solution.py:259
  497.8 37.1 %reduce-scatter.7.cloned.1.call-done = bf16[256,1024]{1,0:T(8,128)(2,1)} async-done(((bf16[1024,1024]{1,0:T(8,128)(2,1)}), bf16[256,1024]{1,0:T(8,128)(2,1)}) %reduce-scatter.7.cloned.1.call-update) | async-done | bytes 524304 | tf_op jit(solution)/shard_map/reduce_scatter | solution.py:258
  537.7 39.9 %psum.30 = f32[13312]{0:T(1024)S(1)} all-reduce(f32[13312]{0:T(1024)S(1)} %constant_dynamic-update-slice_fusion), channel_id=1, replica_groups=mesh['dp'=4,'fsdp'=8] {'dp','fsdp'}, use_global_device_ids=true, to_apply=%region_33.34 | all-reduce | flops 13312 | bytes 106496 | tf_op jit(solution)/shard_map/psum | solution.py:289
  578.3 3.4 stack.92
  581.7 3.3 stack.81
  584.9 3.0 copy.111
  588.0 14.7 %all-reduce.1 = (f32[5]{0:T(128)S(1)}, f32[5]{0:T(128)S(1)}) all-reduce(f32[5]{0:T(128)S(1)} %stack.81, f32[5]{0:T(128)S(1)} %stack.92), channel_id=1, replica_groups=mesh['dp'=4,'fsdp'=8] {'fsdp'}, use_global_device_ids=true, to_apply=%region_16.17 | all-reduce | flops 10 | bytes 80 | tf_op jit(solution)/shard_map/psum | solution.py:323
  610.3 4.2 multiply_subtract_fusion.2
  614.5 3.0 copy.109
  618.7 5.4 multiply_subtract_fusion
  (246 shorter events, 80.4 us)
Async XLA Ops:
  7.2 40.8 %all-gather.13.cloned.1.call-start = ((), (), s32[]{:S(2)}) async-start(), calls=%async_computation.6 | async-start | bytes 2621440 | tf_op jit(solution)/shard_map/all_gather | solution.py:240
  7.9 69.4 %all-gather.15.cloned.1.call-start = ((), (), s32[]{:S(2)}) async-start(), calls=%async_computation.7 | async-start | bytes 1769472 | tf_op jit(solution)/shard_map/all_gather | solution.py:238
  8.0 5.7 copy-start.1
  12.9 102.3 %all-gather.23.cloned.1.call-start = ((), (), s32[]{:S(2)}) async-start(), calls=%async_computation.12 | async-start | bytes 2621440 | tf_op jit(solution)/shard_map/all_gather | solution.py:241
  13.6 21.3 %copy-start.58 = (u32[32]{0:T(128)S(1)}, u32[32]{0:T(128)}, u32[]{:S(2)}) copy-start(u32[32]{0:T(128)} %constant.166) | copy-start | bytes 388
  13.6 133.0 %all-gather.19.cloned.1.call-start = ((), (), s32[]{:S(2)}) async-start(), calls=%async_computation.9 | async-start | bytes 2359296 | tf_op jit(solution)/shard_map/all_gather | solution.py:238
  15.2 161.6 %all-gather.21.cloned.1.call-start = ((), (), s32[]{:S(2)}) async-start(), calls=%async_computation.10 | async-start | bytes 2359296 | tf_op jit(solution)/shard_map/all_gather | solution.py:238
  17.1 197.8 %reduce-scatter.13.cloned.1.call-start = ((), (), s32[]{:S(2)}) async-start(), calls=%async_computation.15 | async-start | bytes 2359296 | tf_op jit(solution)/shard_map/reduce_scatter | solution.py:305
  33.5 18.1 %copy-start.38 = (f32[1024]{0:T(1024)}, f32[1024]{0:T(1024)S(1)}, u32[]{:S(2)}) copy-start(f32[1024]{0:T(1024)S(1)} %get-tuple-element.107) | copy-start | bytes 12292
  33.5 18.1 %copy-start.40 = (f32[1024]{0:T(1024)}, f32[1024]{0:T(1024)S(1)}, u32[]{:S(2)}) copy-start(f32[1024]{0:T(1024)S(1)} %get-tuple-element.106) | copy-start | bytes 12292
  33.5 18.1 %copy-start.47 = (f32[1024]{0:T(1024)}, f32[1024]{0:T(1024)S(1)}, u32[]{:S(2)}) copy-start(f32[1024]{0:T(1024)S(1)} %get-tuple-element.105) | copy-start | bytes 12292
  106.7 5.3 copy-start.28
  106.7 5.3 copy-start.30
  106.7 5.3 copy-start.32
  106.7 5.3 copy-start.34
  106.7 5.3 copy-start.25
  120.6 138.9 %all-reduce.4.cloned.1.call-start = ((), (), s32[]{:S(2)}) async-start(), calls=%async_computation.16 | async-start | bytes 524288 | tf_op jit(solution)/shard_map/psum | solution.py:304
  214.9 83.4 %reduce-scatter.15.cloned.1.call-start = ((), (), s32[]{:S(2)}) async-start(), calls=%async_computation.17 | async-start | bytes 2359296 | tf_op jit(solution)/shard_map/reduce_scatter | solution.py:298
  220.9 114.8 %reduce-scatter.17.cloned.1.call-start = ((), (), s32[]{:S(2)}) async-start(), calls=%async_computation.18 | async-start | bytes 2359296 | tf_op jit(solution)/shard_map/reduce_scatter | solution.py:298
  227.1 32.3 %copy-start.14 = (f32[128,1024]{1,0:T(8,128)S(1)}, f32[128,1024]{1,0:T(8,128)}, u32[]{:S(2)}) copy-start(f32[128,1024]{1,0:T(8,128)} %param.22) | copy-start | bytes 1572868
  227.1 32.3 %copy-start.27 = (f32[128,1024]{1,0:T(8,128)S(1)}, f32[128,1024]{1,0:T(8,128)}, u32[]{:S(2)}) copy-start(f32[128,1024]{1,0:T(8,128)} %param.32) | copy-start | bytes 1572868
  227.2 138.3 %all-gather.17.cloned.1.call-start = ((), (), s32[]{:S(2)}) async-start(), calls=%async_computation.8 | async-start | bytes 2359296 | tf_op jit(solution)/shard_map/all_gather | solution.py:238
  262.6 150.9 %all-gather.25.cloned.1.call-start = ((), (), s32[]{:S(2)}) async-start(), calls=%async_computation.19 | async-start | bytes 1310720 | tf_op jit(solution)/shard_map/all_gather | solution.py:299
  298.3 123.9 %all-gather.27.cloned.1.call-start = ((), (), s32[]{:S(2)}) async-start(), calls=%async_computation.20 | async-start | bytes 1310720 | tf_op jit(solution)/shard_map/all_gather | solution.py:299
  335.8 123.7 %reduce-scatter.11.cloned.1.call-start = ((), (), s32[]{:S(2)}) async-start(), calls=%async_computation.14 | async-start | bytes 1769472 | tf_op jit(solution)/shard_map/reduce_scatter | solution.py:298
  387.0 5.2 copy-start.39
  387.0 5.2 copy-start.48
  387.0 5.2 copy-start.50
  387.0 5.2 copy-start.52
  387.0 109.3 %reduce-scatter.9.cloned.1.call-start = ((), (), s32[]{:S(2)}) async-start(), calls=%async_computation.13 | async-start | bytes 2621440 | tf_op jit(solution)/shard_map/reduce_scatter | solution.py:259
  387.5 4.8 copy-start.23
  387.5 4.8 copy-start.57
  396.5 138.4 %reduce-scatter.7.cloned.1.call-start = ((), (), s32[]{:S(2)}) async-start(), calls=%async_computation.11 | async-start | bytes 2621440 | tf_op jit(solution)/shard_map/reduce_scatter | solution.py:258
  403.1 4.7 copy-start.20
  419.0 10.8 %copy-start.2 = (f32[128,4096]{1,0:T(8,128)S(1)}, f32[128,4096]{1,0:T(8,128)}, u32[]{:S(2)}) copy-start(f32[128,4096]{1,0:T(8,128)} %param.23) | copy-start | bytes 6291460
  422.2 7.5 %copy-start.5 = (f32[128,4096]{1,0:T(8,128)S(1)}, f32[128,4096]{1,0:T(8,128)}, u32[]{:S(2)}) copy-start(f32[128,4096]{1,0:T(8,128)} %reshape.352) | copy-start | bytes 6291460
  422.2 7.5 %copy-start.11 = (f32[128,4096]{1,0:T(8,128)S(1)}, f32[128,4096]{1,0:T(8,128)}, u32[]{:S(2)}) copy-start(f32[128,4096]{1,0:T(8,128)} %param.33) | copy-start | bytes 6291460
  422.2 7.5 %copy-start.12 = (f32[128,4096]{1,0:T(8,128)S(1)}, f32[128,4096]{1,0:T(8,128)}, u32[]{:S(2)}) copy-start(f32[128,4096]{1,0:T(8,128)} %param.28) | copy-start | bytes 6291460
  485.8 49.2 %copy-start.18 = (bf16[1,256,1024]{2,1,0:T(8,128)(2,1)S(1)}, bf16[1,256,1024]{2,1,0:T(8,128)(2,1)}, u32[]{:S(2)}) copy-start(bf16[1,256,1024]{2,1,0:T(8,128)(2,1)} %param.19) | copy-start | bytes 1572868
  485.8 49.2 %copy-start.45 = (f32[1024]{0:T(1024)S(1)}, f32[1024]{0:T(1024)}, u32[]{:S(2)}) copy-start(f32[1024]{0:T(1024)} %get-tuple-element.102) | copy-start | bytes 12292
  485.8 49.2 %copy-start.46 = (f32[1024]{0:T(1024)S(1)}, f32[1024]{0:T(1024)}, u32[]{:S(2)}) copy-start(f32[1024]{0:T(1024)} %get-tuple-element.103) | copy-start | bytes 12292
  488.9 88.7 %copy-start.37 = (f32[1664]{0:T(1024)S(1)}, f32[1664]{0:T(1024)}, u32[]{:S(2)}) copy-start(f32[1664]{0:T(1024)} %param.25) | copy-start | bytes 19972
  488.9 88.7 %copy-start.54 = (f32[1664]{0:T(1024)S(1)}, f32[1664]{0:T(1024)}, u32[]{:S(2)}) copy-start(f32[1664]{0:T(1024)} %param.35) | copy-start | bytes 19972
  488.9 88.7 %copy-start.55 = (f32[1664]{0:T(1024)S(1)}, f32[1664]{0:T(1024)}, u32[]{:S(2)}) copy-start(f32[1664]{0:T(1024)} %param.30) | copy-start | bytes 19972
  578.3 39.8 %copy-start.42 = (f32[1664]{0:T(1024)}, f32[1664]{0:T(1024)S(1)}, u32[]{:S(2)}) copy-start(f32[1664]{0:T(1024)S(1)} %get-tuple-element.75) | copy-start | bytes 19972
  578.3 39.8 %copy-start.43 = (f32[1664]{0:T(1024)}, f32[1664]{0:T(1024)S(1)}, u32[]{:S(2)}) copy-start(f32[1664]{0:T(1024)S(1)} %get-tuple-element.76) | copy-start | bytes 19972
  618.7 5.4 copy-start.6
  618.7 5.4 copy-start.7
  (26 other events, 58.7 us)
Sparse Core Ops, SparseCore 0:
  9.9 38.0 all-gather.12
  50.2 27.1 all-gather.14
  79.2 34.4 all-gather.22
  115.7 30.8 all-gather.18
  148.6 28.1 all-gather.20
  179.5 35.2 reduce-scatter.12
  217.8 41.6 all-reduce.3
  262.4 35.7 reduce-scatter.14
  301.2 34.4 reduce-scatter.16
  337.8 27.6 all-gather.16
  367.5 26.1 all-gather.24
  395.5 26.6 all-gather.26
  425.2 34.1 reduce-scatter.10
  463.1 33.1 reduce-scatter.8
  499.7 35.1 reduce-scatter.6
where the time goes:
time: 638 us; the launch traced here: 634 us
  waiting for transfers between devices  299 us (47%)
  blocking collectives  93.2 us (15%)
  local copies, waits for them, and re-layouts  80.2 us (13%)
  matrix products  78.1 us (12%)
  other arithmetic  60.6 us (9%)
  between operations  22 us (3%)
    reduce_scatter x3, waiting for transfers between devices, to_owner(): own = lax.psum_scatter(term, 'fsdp', scatter_dimension=0, tiled=True)  95.5 us
    all_gather x4, waiting for transfers between devices, over_shards(): return lax.all_gather(own, 'fsdp', axis=0, tiled=True)  90 us
    psum x1, blocking collectives, local_split(): small_sum = lax.psum(small_grad, ('dp', 'fsdp'))  39.9 us
    reduce_scatter x1, waiting for transfers between devices, local_split(): out_sum = lax.psum_scatter(out_part, 'dp', scatter_dimension=0, tiled=True)  37.1 us
    unnamed x143, local copies, waits for them, and re-layouts  33.9 us
    psum x1, waiting for transfers between devices, local_split(): lax.psum(lax.psum_scatter(out_wide, 'fsdp', scatter_dimension=0, tiled=Tr...  32.3 us
    reduce_scatter x1, waiting for transfers between devices, local_split(): lax.psum_scatter(out_wide, 'fsdp', scatter_dimension=0, tiled=True)  30 us
    reduce_sum x6, other arithmetic, local_squares(): return jnp.stack([jnp.sum(array_in * array_in) for array_in in arrays])  21.3 us
  transfers between devices with their start and end apart: 15, of which 13 were waited for; matrix products, arithmetic and copies ran while one was open for 28% of the time, Pallas kernels for 0%

commit v1 on v0

--- a/solution.py
+++ b/solution.py
@@ -286,7 +286,9 @@
             back_total,
         ]
     )
-    small_sum = lax.psum(small_grad, ("dp", "fsdp"))
+    small_sum = small_grad
+    for mesh_axis in ("fsdp", "dp"):
+        small_sum = lax.psum(small_sum, mesh_axis)
     small_rows = small_master.shape[0]
     small_sum = lax.dynamic_slice_in_dim(small_sum, shard * small_rows, small_rows)
     qkv_term, out_term, up_term, down_term = terms

time: 638 us -> 643 us (level)
    psum x1 -> x2, blocking collectives: 39.9 us -> 45.1 us  [local_split(): small_sum = lax.psum(small_sum, mesh_axis)]
where the time goes in v1:
time: 643 us; the launch traced here: 639 us
  waiting for transfers between devices  299 us (47%)
  blocking collectives  97.5 us (15%)
  local copies, waits for them, and re-layouts  80.1 us (12%)
  matrix products  78.2 us (12%)
  other arithmetic  60.6 us (9%)
  between operations  22.2 us (3%)
    reduce_scatter x3, waiting for transfers between devices, to_owner(): own = lax.psum_scatter(term, 'fsdp', scatter_dimension=0, tiled=True)  95.6 us
    all_gather x4, waiting for transfers between devices, over_shards(): return lax.all_gather(own, 'fsdp', axis=0, tiled=True)  90 us
    psum x2, blocking collectives, local_split(): small_sum = lax.psum(small_sum, mesh_axis)  45.1 us
    reduce_scatter x1, waiting for transfers between devices, local_split(): out_sum = lax.psum_scatter(out_part, 'dp', scatter_dimension=0, tiled=True)  37.1 us
    unnamed x143, local copies, waits for them, and re-layouts  33.9 us
    psum x1, waiting for transfers between devices, local_split(): lax.psum(lax.psum_scatter(out_wide, 'fsdp', scatter_dimension=0, tiled=Tr...  32.3 us
    reduce_scatter x1, waiting for transfers between devices, local_split(): lax.psum_scatter(out_wide, 'fsdp', scatter_dimension=0, tiled=True)  30 us
    reduce_sum x6, other arithmetic, local_squares(): return jnp.stack([jnp.sum(array_in * array_in) for array_in in arrays])  21.3 us
  transfers between devices with their start and end apart: 15, of which 13 were waited for; matrix products, arithmetic and copies ran while one was open for 28% of the time, Pallas kernels for 0%

profile of v1, /device:TPU:0, one launch (start us, length us, event | category | flops | bytes accessed | tf_op | source)
XLA Modules:
  0.0 638.7 jit_solution(6188957719658167694)
XLA Ops:
  8.0 3.2 copy.87
  17.1 15.7 %all-gather.3 = bf16[8,1,1664]{2,1,0:T(2,128)(2,1)S(1)} all-gather(bf16[1,1,1664]{2,1,0:T(2,128)(2,1)S(1)} %reshape.376), channel_id=1, replica_groups=mesh['dp'=4,'fsdp'=8] {'fsdp'}, dimensions={0}, use_global_device_ids=true | all-gather | bytes 29952 | tf_op jit(solution)/shard_map/all_gather | solution.py:238
  36.3 8.1 %all-reduce = s32[4]{0:T(128)S(1)} all-reduce(s32[4]{0:T(128)S(1)} %dynamic-update-slice), channel_id=1, replica_groups=mesh['dp'=4,'fsdp'=8] {'dp'}, use_global_device_ids=true, to_apply=%add | all-reduce | flops 4 | bytes 32
  54.4 23.0 %all-gather.15.cloned.1.call-done = bf16[1024,768]{0,1:T(8,128)(2,1)} async-done(((bf16[128,768]{0,1:T(8,128)(2,1)}), bf16[1024,768]{0,1:T(8,128)(2,1)}) %all-gather.15.cloned.1.call-update) | async-done | bytes 1572880 | tf_op jit(solution)/shard_map/all_gather | solution.py:238
  77.4 5.6 convolution_add_fusion
  82.9 6.4 %reshape.381 = f32[4,256,3,4,64]{4,3,2,1,0:T(4,128)} reshape(f32[1024,768]{1,0:T(8,128)} %convolution_add_fusion) | data formatting | bytes 6291456 | tf_op jit(solution)/shard_map/reshape | solution.py:127
  91.3 4.5 fusion.75
  106.7 5.3 fusion.79
  121.5 3.4 fusion.10
  124.9 21.7 %all-gather.19.cloned.1.call-done = bf16[1024,1024]{0,1:T(8,128)(2,1)} async-done(((bf16[128,1024]{0,1:T(8,128)(2,1)}), bf16[1024,1024]{0,1:T(8,128)(2,1)}) %all-gather.19.cloned.1.call-update) | async-done | bytes 2097168 | tf_op jit(solution)/shard_map/all_gather | solution.py:238
  146.6 14.6 %fusion.3 = (bf16[1024,1024]{1,0:T(8,128)(2,1)}, f32[1024,1024]{1,0:T(8,128)}) fusion(f32[1024]{0:T(1024)S(1)} %bitcast.220, bf16[1024,1024]{1,0:T(8,128)(2,1)} %get-tuple-element.89, bf16[1024,1024]{0,1:T(8,128)(2,1)} %all-gather.19.cloned.1.call-done), kind=kOutput, calls=%fused_computation.5 | convolution fusion | flops 2216689664 | bytes 10489856 | tf_op jit(solution)/shard_map/dot_general | solution.py:144
  161.2 15.7 %all-gather.21.cloned.1.call-done = bf16[1024,1024]{1,0:T(8,128)(2,1)} async-done(((bf16[128,1024]{1,0:T(8,128)(2,1)}), bf16[1024,1024]{1,0:T(8,128)(2,1)}) %all-gather.21.cloned.1.call-update) | async-done | bytes 2097168 | tf_op jit(solution)/shard_map/all_gather | solution.py:238
  176.8 8.0 %convert_reduce_fusion = (f32[1024]{0:T(1024)}, bf16[1024,1024]{1,0:T(8,128)(2,1)}) fusion(f32[1024,1024]{1,0:T(8,128)} %get-tuple-element.138, f32[1024]{0:T(1024)S(1)} %bitcast.221, bf16[1024,1024]{1,0:T(8,128)(2,1)} %fusion.10, bf16[1024,1024]{1,0:T(8,128)(2,1)} %all-gather.21.cloned.1.call-done), kind=kOutput, calls=%fused_computation.16 | convolution fusion | flops 2161114112 | bytes 10493952 | tf_op jit(solution)/shard_map/dot_general | solution.py:77
  184.9 30.0 %reduce-scatter.13.cloned.1.call-done = bf16[128,1024]{1,0:T(8,128)(2,1)} async-done(((bf16[1024,1024]{1,0:T(8,128)(2,1)}), bf16[128,1024]{1,0:T(8,128)(2,1)}) %reduce-scatter.13.cloned.1.call-update) | async-done | bytes 262160 | tf_op jit(solution)/shard_map/reduce_scatter | solution.py:307
  214.9 5.9 convolution_convert_fusion.1
  221.2 6.0 convolution_convert_fusion
  227.2 32.3 %all-reduce.4.cloned.1.call-done = bf16[128,1024]{1,0:T(8,128)(2,1)} async-done(((bf16[128,1024]{1,0:T(8,128)(2,1)}), bf16[128,1024]{1,0:T(8,128)(2,1)}) %all-reduce.4.cloned.1.call-update) | async-done | bytes 262160 | tf_op jit(solution)/shard_map/psum | solution.py:306
  259.5 3.1 multiply_reduce_fusion.10
  262.7 35.6 %reduce-scatter.15.cloned.1.call-done = bf16[128,1024]{1,0:T(8,128)(2,1)} async-done(((bf16[1024,1024]{1,0:T(8,128)(2,1)}), bf16[128,1024]{1,0:T(8,128)(2,1)}) %reduce-scatter.15.cloned.1.call-update) | async-done | bytes 262160 | tf_op jit(solution)/shard_map/reduce_scatter | solution.py:300
  298.4 2.8 add_convert_fusion
  301.2 34.5 %reduce-scatter.17.cloned.1.call-done = bf16[128,1024]{1,0:T(8,128)(2,1)} async-done(((bf16[1024,1024]{1,0:T(8,128)(2,1)}), bf16[128,1024]{1,0:T(8,128)(2,1)}) %reduce-scatter.17.cloned.1.call-update) | async-done | bytes 262160 | tf_op jit(solution)/shard_map/reduce_scatter | solution.py:300
  335.8 29.7 %all-gather.17.cloned.1.call-done = bf16[1024,1024]{1,0:T(8,128)(2,1)} async-done(((bf16[128,1024]{1,0:T(8,128)(2,1)}), bf16[1024,1024]{1,0:T(8,128)(2,1)}) %all-gather.17.cloned.1.call-update) | async-done | bytes 2097168 | tf_op jit(solution)/shard_map/all_gather | solution.py:238
  365.5 3.2 convolution_convert_fusion.4
  372.0 3.6 multiply_reduce_fusion.2
  384.0 3.0 convolution_convert_fusion.2
  387.5 4.7 fusion.81
  392.3 4.3 multiply_reduce_fusion.1
  399.6 3.1 copy.105
  403.1 4.6 fusion.80
  407.8 3.1 add_convert_fusion.2
  419.0 3.3 all-gather.27.cloned.1.call-done
  422.3 7.5 %multiply_reduce_fusion.4 = (f32[]{:T(128)}, f32[]{:T(128)}, f32[512,1024]{1,0:T(8,128)}, f32[512,1024]{1,0:T(8,128)}) fusion(f32[512,1024]{1,0:T(8,128)} %param.24, bf16[512,1024]{1,0:T(8,128)(2,1)} %all-gather.27.cloned.1.call-done, f32[512,1024]{1,0:T(8,128)} %param.34, f32[512,1024]{1,0:T(8,128)} %param.29), kind=kLoop, calls=%fused_computation.61 | loop fusion | flops 7864318 | bytes 11534344 | tf_op jit(solution)/shard_map/reduce_sum | solution.py:89
  429.8 4.1 multiply_reduce_fusion.5
  434.1 25.4 %reduce-scatter.11.cloned.1.call-done = bf16[128,768]{1,0:T(8,128)(2,1)} async-done(((bf16[1024,768]{1,0:T(8,128)(2,1)}), bf16[128,768]{1,0:T(8,128)(2,1)}) %reduce-scatter.11.cloned.1.call-update) | async-done | bytes 196624 | tf_op jit(solution)/shard_map/reduce_scatter | solution.py:300
  459.5 14.9 %all-gather = bf16[512,768]{1,0:T(8,128)(2,1)S(1)} all-gather(bf16[128,768]{1,0:T(8,128)(2,1)} %reduce-scatter.11.cloned.1.call-done), channel_id=2, replica_groups=mesh['dp'=4,'fsdp'=8] {'dp'}, dimensions={0}, use_global_device_ids=true | all-gather | bytes 983040 | tf_op jit(solution)/shard_map/all_gather | solution.py:301
  481.0 4.9 multiply_reduce_fusion.8
  485.8 3.1 copy.110
  488.9 7.5 %reduce-scatter.9.cloned.1.call-done = bf16[256,1024]{1,0:T(8,128)(2,1)} async-done(((bf16[1024,1024]{1,0:T(8,128)(2,1)}), bf16[256,1024]{1,0:T(8,128)(2,1)}) %reduce-scatter.9.cloned.1.call-update) | async-done | bytes 524304 | tf_op jit(solution)/shard_map/reduce_scatter | solution.py:259
  497.8 37.1 %reduce-scatter.7.cloned.1.call-done = bf16[256,1024]{1,0:T(8,128)(2,1)} async-done(((bf16[1024,1024]{1,0:T(8,128)(2,1)}), bf16[256,1024]{1,0:T(8,128)(2,1)}) %reduce-scatter.7.cloned.1.call-update) | async-done | bytes 524304 | tf_op jit(solution)/shard_map/reduce_scatter | solution.py:258
  537.7 29.0 %psum.37 = f32[13312]{0:T(1024)S(1)} all-reduce(f32[13312]{0:T(1024)S(1)} %constant_dynamic-update-slice_fusion), channel_id=1, replica_groups=mesh['dp'=4,'fsdp'=8] {'fsdp'}, use_global_device_ids=true, to_apply=%region_33.34 | all-reduce | flops 13312 | bytes 106496 | tf_op jit(solution)/shard_map/psum | solution.py:291
  566.7 16.1 %psum.38 = f32[13312]{0:T(1024)S(1)} all-reduce(f32[13312]{0:T(1024)S(1)} %psum.37), channel_id=1, replica_groups=mesh['dp'=4,'fsdp'=8] {'dp'}, use_global_device_ids=true, to_apply=%region_34.35 | all-reduce | flops 13312 | bytes 106496 | tf_op jit(solution)/shard_map/psum | solution.py:291
  583.5 3.3 stack.92
  586.9 3.2 stack.81
  590.1 3.0 copy.111
  593.1 13.8 %all-reduce.1 = (f32[5]{0:T(128)S(1)}, f32[5]{0:T(128)S(1)}) all-reduce(f32[5]{0:T(128)S(1)} %stack.81, f32[5]{0:T(128)S(1)} %stack.92), channel_id=1, replica_groups=mesh['dp'=4,'fsdp'=8] {'fsdp'}, use_global_device_ids=true, to_apply=%region_16.17 | all-reduce | flops 10 | bytes 80 | tf_op jit(solution)/shard_map/psum | solution.py:325
  614.8 4.2 multiply_subtract_fusion.2
  619.0 3.0 copy.109
  623.2 5.4 multiply_subtract_fusion
  (247 shorter events, 83.2 us)
Async XLA Ops:
  7.2 40.8 %all-gather.13.cloned.1.call-start = ((), (), s32[]{:S(2)}) async-start(), calls=%async_computation.6 | async-start | bytes 2621440 | tf_op jit(solution)/shard_map/all_gather | solution.py:240
  7.9 69.4 %all-gather.15.cloned.1.call-start = ((), (), s32[]{:S(2)}) async-start(), calls=%async_computation.7 | async-start | bytes 1769472 | tf_op jit(solution)/shard_map/all_gather | solution.py:238
  8.0 5.7 copy-start.1
  12.9 102.3 %all-gather.23.cloned.1.call-start = ((), (), s32[]{:S(2)}) async-start(), calls=%async_computation.12 | async-start | bytes 2621440 | tf_op jit(solution)/shard_map/all_gather | solution.py:241
  13.6 21.3 %copy-start.58 = (u32[32]{0:T(128)S(1)}, u32[32]{0:T(128)}, u32[]{:S(2)}) copy-start(u32[32]{0:T(128)} %constant.166) | copy-start | bytes 388
  13.6 133.0 %all-gather.19.cloned.1.call-start = ((), (), s32[]{:S(2)}) async-start(), calls=%async_computation.9 | async-start | bytes 2359296 | tf_op jit(solution)/shard_map/all_gather | solution.py:238
  15.2 161.6 %all-gather.21.cloned.1.call-start = ((), (), s32[]{:S(2)}) async-start(), calls=%async_computation.10 | async-start | bytes 2359296 | tf_op jit(solution)/shard_map/all_gather | solution.py:238
  17.1 197.8 %reduce-scatter.13.cloned.1.call-start = ((), (), s32[]{:S(2)}) async-start(), calls=%async_computation.15 | async-start | bytes 2359296 | tf_op jit(solution)/shard_map/reduce_scatter | solution.py:307
  33.5 18.1 %copy-start.38 = (f32[1024]{0:T(1024)}, f32[1024]{0:T(1024)S(1)}, u32[]{:S(2)}) copy-start(f32[1024]{0:T(1024)S(1)} %get-tuple-element.107) | copy-start | bytes 12292
  33.5 18.1 %copy-start.40 = (f32[1024]{0:T(1024)}, f32[1024]{0:T(1024)S(1)}, u32[]{:S(2)}) copy-start(f32[1024]{0:T(1024)S(1)} %get-tuple-element.106) | copy-start | bytes 12292
  33.5 18.1 %copy-start.47 = (f32[1024]{0:T(1024)}, f32[1024]{0:T(1024)S(1)}, u32[]{:S(2)}) copy-start(f32[1024]{0:T(1024)S(1)} %get-tuple-element.105) | copy-start | bytes 12292
  106.7 5.3 copy-start.28
  106.7 5.3 copy-start.30
  106.7 5.3 copy-start.32
  106.7 5.3 copy-start.34
  106.7 5.3 copy-start.25
  120.6 138.9 %all-reduce.4.cloned.1.call-start = ((), (), s32[]{:S(2)}) async-start(), calls=%async_computation.16 | async-start | bytes 524288 | tf_op jit(solution)/shard_map/psum | solution.py:306
  214.9 83.4 %reduce-scatter.15.cloned.1.call-start = ((), (), s32[]{:S(2)}) async-start(), calls=%async_computation.17 | async-start | bytes 2359296 | tf_op jit(solution)/shard_map/reduce_scatter | solution.py:300
  220.9 114.9 %reduce-scatter.17.cloned.1.call-start = ((), (), s32[]{:S(2)}) async-start(), calls=%async_computation.18 | async-start | bytes 2359296 | tf_op jit(solution)/shard_map/reduce_scatter | solution.py:300
  227.1 32.4 %copy-start.14 = (f32[128,1024]{1,0:T(8,128)S(1)}, f32[128,1024]{1,0:T(8,128)}, u32[]{:S(2)}) copy-start(f32[128,1024]{1,0:T(8,128)} %param.22) | copy-start | bytes 1572868
  227.1 32.4 %copy-start.27 = (f32[128,1024]{1,0:T(8,128)S(1)}, f32[128,1024]{1,0:T(8,128)}, u32[]{:S(2)}) copy-start(f32[128,1024]{1,0:T(8,128)} %param.32) | copy-start | bytes 1572868
  227.2 138.4 %all-gather.17.cloned.1.call-start = ((), (), s32[]{:S(2)}) async-start(), calls=%async_computation.8 | async-start | bytes 2359296 | tf_op jit(solution)/shard_map/all_gather | solution.py:238
  262.6 150.9 %all-gather.25.cloned.1.call-start = ((), (), s32[]{:S(2)}) async-start(), calls=%async_computation.19 | async-start | bytes 1310720 | tf_op jit(solution)/shard_map/all_gather | solution.py:301
  298.3 123.9 %all-gather.27.cloned.1.call-start = ((), (), s32[]{:S(2)}) async-start(), calls=%async_computation.20 | async-start | bytes 1310720 | tf_op jit(solution)/shard_map/all_gather | solution.py:301
  335.8 123.7 %reduce-scatter.11.cloned.1.call-start = ((), (), s32[]{:S(2)}) async-start(), calls=%async_computation.14 | async-start | bytes 1769472 | tf_op jit(solution)/shard_map/reduce_scatter | solution.py:300
  387.0 5.2 copy-start.39
  387.0 5.2 copy-start.48
  387.0 5.2 copy-start.50
  387.0 5.2 copy-start.52
  387.0 109.3 %reduce-scatter.9.cloned.1.call-start = ((), (), s32[]{:S(2)}) async-start(), calls=%async_computation.13 | async-start | bytes 2621440 | tf_op jit(solution)/shard_map/reduce_scatter | solution.py:259
  387.5 4.8 copy-start.23
  387.5 4.8 copy-start.57
  396.6 138.4 %reduce-scatter.7.cloned.1.call-start = ((), (), s32[]{:S(2)}) async-start(), calls=%async_computation.11 | async-start | bytes 2621440 | tf_op jit(solution)/shard_map/reduce_scatter | solution.py:258
  403.1 4.7 copy-start.20
  419.0 10.8 %copy-start.2 = (f32[128,4096]{1,0:T(8,128)S(1)}, f32[128,4096]{1,0:T(8,128)}, u32[]{:S(2)}) copy-start(f32[128,4096]{1,0:T(8,128)} %param.23) | copy-start | bytes 6291460
  422.2 7.6 %copy-start.5 = (f32[128,4096]{1,0:T(8,128)S(1)}, f32[128,4096]{1,0:T(8,128)}, u32[]{:S(2)}) copy-start(f32[128,4096]{1,0:T(8,128)} %reshape.352) | copy-start | bytes 6291460
  422.2 7.6 %copy-start.11 = (f32[128,4096]{1,0:T(8,128)S(1)}, f32[128,4096]{1,0:T(8,128)}, u32[]{:S(2)}) copy-start(f32[128,4096]{1,0:T(8,128)} %param.33) | copy-start | bytes 6291460
  422.3 7.6 %copy-start.12 = (f32[128,4096]{1,0:T(8,128)S(1)}, f32[128,4096]{1,0:T(8,128)}, u32[]{:S(2)}) copy-start(f32[128,4096]{1,0:T(8,128)} %param.28) | copy-start | bytes 6291460
  485.8 49.2 %copy-start.18 = (bf16[1,256,1024]{2,1,0:T(8,128)(2,1)S(1)}, bf16[1,256,1024]{2,1,0:T(8,128)(2,1)}, u32[]{:S(2)}) copy-start(bf16[1,256,1024]{2,1,0:T(8,128)(2,1)} %param.19) | copy-start | bytes 1572868
  485.8 49.2 %copy-start.45 = (f32[1024]{0:T(1024)S(1)}, f32[1024]{0:T(1024)}, u32[]{:S(2)}) copy-start(f32[1024]{0:T(1024)} %get-tuple-element.102) | copy-start | bytes 12292
  485.8 49.2 %copy-start.46 = (f32[1024]{0:T(1024)S(1)}, f32[1024]{0:T(1024)}, u32[]{:S(2)}) copy-start(f32[1024]{0:T(1024)} %get-tuple-element.103) | copy-start | bytes 12292
  488.9 93.9 %copy-start.37 = (f32[1664]{0:T(1024)S(1)}, f32[1664]{0:T(1024)}, u32[]{:S(2)}) copy-start(f32[1664]{0:T(1024)} %param.25) | copy-start | bytes 19972
  488.9 93.9 %copy-start.54 = (f32[1664]{0:T(1024)S(1)}, f32[1664]{0:T(1024)}, u32[]{:S(2)}) copy-start(f32[1664]{0:T(1024)} %param.35) | copy-start | bytes 19972
  488.9 93.9 %copy-start.55 = (f32[1664]{0:T(1024)S(1)}, f32[1664]{0:T(1024)}, u32[]{:S(2)}) copy-start(f32[1664]{0:T(1024)} %param.30) | copy-start | bytes 19972
  583.5 39.0 %copy-start.42 = (f32[1664]{0:T(1024)}, f32[1664]{0:T(1024)S(1)}, u32[]{:S(2)}) copy-start(f32[1664]{0:T(1024)S(1)} %get-tuple-element.75) | copy-start | bytes 19972
  583.5 39.0 %copy-start.43 = (f32[1664]{0:T(1024)}, f32[1664]{0:T(1024)S(1)}, u32[]{:S(2)}) copy-start(f32[1664]{0:T(1024)S(1)} %get-tuple-element.76) | copy-start | bytes 19972
  623.2 5.4 copy-start.6
  623.2 5.4 copy-start.7
  (26 other events, 58.7 us)
Sparse Core Ops, SparseCore 0:
  9.9 38.0 all-gather.12
  50.2 27.1 all-gather.14
  79.2 34.4 all-gather.22
  115.7 30.8 all-gather.18
  148.6 28.1 all-gather.20
  179.5 35.2 reduce-scatter.12
  217.8 41.6 all-reduce.3
  262.5 35.7 reduce-scatter.14
  301.3 34.4 reduce-scatter.16
  337.9 27.6 all-gather.16
  367.5 26.1 all-gather.24
  395.5 26.6 all-gather.26
  425.2 34.1 reduce-scatter.10
  463.1 33.1 reduce-scatter.8
  499.7 35.1 reduce-scatter.6
